TPU v7x, 256 devices: a whole 4x4x8 slice. The times are simulated.
256 devices in a mesh: row: 16 (over z, core), col: 16 (over y, x).
Axes of the slice: x: 4, y: 4, z: 8, core: 2. Of those that a mesh axis runs over, the one named last changes fastest.
Arguments:
- inverse: float32 [5, 16, 5, 16, 256, 256], P(None, 'row', None, 'col')
- struct_first: int32 [32], replicated, may hold values from 0 to 79, as said below
- struct_second: int32 [16], replicated, may hold values from 0 to 79, as said below
- factor_first: float32 [32, 256, 256], P('row'), may hold values from -0.25 to 0.25
- factor_second: float32 [16, 256, 256], P('row'), may hold values from -0.25 to 0.25
- link_factor: float32 [256, 256], replicated, may hold values from -0.375 to 0.375
- dinv_first: float32 [256, 256], replicated, may hold values from -6 to 6
- dinv_second: float32 [256, 256], replicated, may hold values from -6 to 6
Outputs:
- column_first: float32 [5, 16, 256, 256], P(None, 'row', None, 'col')
- diag_first: float32 [256, 256], P(None, 'col')
- column_second: float32 [5, 16, 256, 256], P(None, 'row', None, 'col')
- link_second: float32 [256, 256], P(None, 'col')
- diag_second: float32 [256, 256], P(None, 'col')
Inputs may be any that keep to these rules, and one draw needn't show every extreme that they name: `struct_first`: distinct tile ids. `struct_second`: distinct tile ids, each of them also in struct_first.
All inputs are finite; a program needn't handle non-finite values.
Results may differ from a plain program's by a relative error of at most 0.0001.
Values sent between devices are 32-bit elements; how exact they have to be, the bound alone decides.
A program may use at most 128 MiB of HBM per device.

v0:
```python
import jax
import jax.numpy as jnp
from jax import lax
from jax.sharding import PartitionSpec as P

PRECISE = lax.Precision.HIGHEST


def body(
    inverse,
    struct_first,
    struct_second,
    factor_first,
    factor_second,
    link_factor,
    dinv_first,
    dinv_second,
):
    grid_rows = lax.axis_size("row")
    grid_cols = lax.axis_size("col")
    my_row = lax.axis_index("row")
    my_col = lax.axis_index("col")
    tile_rows, _, tile_cols, _, extent, _ = inverse.shape
    local_inv = inverse.reshape(tile_rows, tile_cols, extent, extent)
    col_width = extent // grid_cols
    offset = my_col * col_width
    col_tiles = jnp.arange(tile_cols, dtype=jnp.int32) * grid_cols + my_col
    row_tiles = jnp.arange(tile_rows, dtype=jnp.int32) * grid_rows + my_row

    def route(factor, tile_ids):
        block_in = lax.all_gather(factor, "row", axis=0, tiled=True)
        pick_col = (tile_ids[None, :] == col_tiles[:, None]).astype(jnp.float32)
        pick_row = (tile_ids[None, :] == row_tiles[:, None]).astype(jnp.float32)
        col_sel = jnp.einsum("bj,jxy->bxy", pick_col, block_in, precision=PRECISE)
        row_sel = jnp.einsum("aj,jxy->axy", pick_row, block_in, precision=PRECISE)
        return (col_sel, row_sel)

    def reduce_cols(stacked):
        summed = lax.psum(stacked, "col")
        return lax.dynamic_slice_in_dim(summed, offset, col_width, 2)

    col_first, row_first = route(factor_first, struct_first)
    product_first = jnp.einsum("abxy,byz->axz", local_inv, col_first, precision=PRECISE)
    panel_first = reduce_cols(product_first)
    owned_first = jnp.any(row_tiles[:, None] == struct_first[None, :], axis=1).astype(jnp.float32)
    column_first = -owned_first[:, None, None] * panel_first
    diag_terms = jnp.einsum("axy,axz->yz", row_first, panel_first, precision=PRECISE)
    diag_first = lax.dynamic_slice_in_dim(dinv_first, offset, col_width, 1) + lax.psum(
        diag_terms, "row"
    )
    col_second, row_second = route(factor_second, struct_second)
    link_rows = lax.dynamic_slice_in_dim(link_factor, offset, col_width, 0)
    product_second = jnp.einsum("abxy,byz->axz", local_inv, col_second, precision=PRECISE)
    product_second = product_second + jnp.einsum(
        "axw,wz->axz", column_first, link_rows, precision=PRECISE
    )
    link_term = jnp.dot(
        diag_first, link_rows, precision=PRECISE, preferred_element_type=jnp.float32
    )
    reduced = reduce_cols(jnp.concatenate([product_second, link_term[None]], axis=0))
    panel_second = reduced[:tile_rows]
    join_share = reduced[tile_rows]
    owned_second = jnp.any(row_tiles[:, None] == struct_second[None, :], axis=1).astype(jnp.float32)
    column_second = -owned_second[:, None, None] * panel_second
    turned_part = jnp.einsum("axw,axz->wz", column_first, row_second, precision=PRECISE)
    second_terms = jnp.einsum("axy,axz->yz", row_second, panel_second, precision=PRECISE)
    turned_sum, second_sum = lax.psum((turned_part, second_terms), "row")
    turned = lax.all_to_all(turned_sum, "col", split_axis=1, concat_axis=0, tiled=True)
    joined = turned + join_share
    link_second = -joined
    diag_second = lax.dynamic_slice_in_dim(dinv_second, offset, col_width, 1) + second_sum
    diag_second = diag_second + jnp.dot(
        link_factor.T, joined, precision=PRECISE, preferred_element_type=jnp.float32
    )
    out_shape = (tile_rows, 1, extent, col_width)
    return (
        column_first.reshape(out_shape),
        diag_first,
        column_second.reshape(out_shape),
        link_second,
        diag_second,
    )


def solution(mesh):
    placed = (
        P(None, "row", None, "col", None, None),
        P(),
        P(),
        P("row", None, None),
        P("row", None, None),
        P(),
        P(),
        P(),
    )
    return jax.shard_map(
        body,
        mesh=mesh,
        in_specs=placed,
        out_specs=(
            P(None, "row", None, "col"),
            P(None, "col"),
            P(None, "row", None, "col"),
            P(None, "col"),
            P(None, "col"),
        ),
        check_vma=False,
    )
```

profile of v0, /device:TPU:2, one launch (start us, length us, event | category | flops | bytes accessed | tf_op | source)
XLA Modules:
  0.0 435.4 jit_solution(15003734028828694786)
XLA Ops:
  7.2 0.0 copy-start
  7.2 0.0 all-gather.3.cloned.1.call-start
  7.2 0.7 all-gather.3.cloned.1.call-update
  7.9 0.0 all-gather.5.cloned.1.call-start
  8.0 0.7 all-gather.5.cloned.1.call-update
  8.7 0.0 all-reduce.4.cloned.1.call-start
  8.7 1.0 constant_dynamic-slice_fusion.1
  9.7 0.1 copy.56
  9.8 0.8 compare_reduce_fusion.1
  10.7 58.0 %all-gather.3.cloned.1.call-done = f32[32,256,256]{2,1,0:T(8,128)} async-done(((f32[2,256,256]{2,1,0:T(8,128)}), f32[32,256,256]{2,1,0:T(8,128)}) %all-gather.3.cloned.1.call-update) | async-done | bytes 8388624 | tf_op jit(solution)/shard_map/all_gather | solution.py:31
  68.7 10.6 %fusion.2 = f32[5,256,256]{2,0,1:T(8,128)S(1)} fusion(f32[32,256,256]{2,1,0:T(8,128)} %all-gather.3.cloned.1.call-done, s32[32]{0:T(128)} %param.9, s32[5]{0:T(128)S(1)} %fusion.62), kind=kOutput, calls=%fused_computation.2 | convolution fusion | flops 125829280 | bytes 9699476 | tf_op jit(solution)/shard_map/bj,jxy->bxy/dot_general | solution.py:34
  79.3 1.5 copy.35
  80.8 0.0 copy-start.4
  80.8 9.9 %fusion.12 = f32[5,256,256]{1,2,0:T(8,128)} fusion(f32[5,1,5,1,256,256]{5,4,3,2,1,0:T(8,128)} %param.8, f32[5,256,256]{1,2,0:T(8,128)} %copy.35), kind=kOutput, calls=%fused_computation.13 | convolution fusion | flops 5033164800 | bytes 9175040 | tf_op jit(solution)/shard_map/abxy,byz->axz/dot_general | solution.py:43
  90.8 0.0 all-reduce.4.cloned.1.call-update
  90.8 10.8 %all-reduce.6.cloned.1.call-start = ((), (), s32[]{:S(2)}) async-start(), calls=%async_computation.4 | async-start | bytes 3145728 | tf_op jit(solution)/shard_map/psum | solution.py:39
  101.6 9.4 %all-gather.5.cloned.1.call-done = f32[16,256,256]{2,1,0:T(8,128)} async-done(((f32[1,256,256]{2,1,0:T(8,128)}), f32[16,256,256]{2,1,0:T(8,128)}) %all-gather.5.cloned.1.call-update) | async-done | bytes 4194320 | tf_op jit(solution)/shard_map/all_gather | solution.py:31
  111.0 0.0 copy-done.4
  111.0 5.8 %fusion.10 = f32[5,256,256]{2,0,1:T(8,128)S(1)} fusion(f32[16,256,256]{2,1,0:T(8,128)} %all-gather.5.cloned.1.call-done, s32[16]{0:T(128)S(1)} %copy-done.4, s32[5]{0:T(128)S(1)} %fusion.62), kind=kOutput, calls=%fused_computation.10 | convolution fusion | flops 62914640 | bytes 5505108 | tf_op jit(solution)/shard_map/bj,jxy->bxy/dot_general | solution.py:34
  116.8 1.5 copy.40
  118.3 0.0 copy-start.3
  118.3 10.0 %fusion.15 = f32[5,256,256]{1,2,0:T(8,128)} fusion(f32[5,1,5,1,256,256]{5,4,3,2,1,0:T(8,128)} %param.8, f32[5,256,256]{1,2,0:T(8,128)} %copy.40), kind=kOutput, calls=%fused_computation.14 | convolution fusion | flops 5033164800 | bytes 9175040 | tf_op jit(solution)/shard_map/abxy,byz->axz/dot_general | solution.py:53
  128.3 0.0 copy-done.3
  128.3 10.7 %fusion = f32[5,256,256]{2,0,1:T(8,128)S(1)} fusion(f32[32,256,256]{2,1,0:T(8,128)} %all-gather.3.cloned.1.call-done, s32[32]{0:T(128)S(1)} %copy-done.3, s32[5]{0:T(128)S(1)} %fusion.63), kind=kOutput, calls=%fused_computation | convolution fusion | flops 125829280 | bytes 9699476 | tf_op jit(solution)/shard_map/aj,jxy->axy/dot_general | solution.py:35
  139.0 71.3 %all-reduce.4.cloned.1.call-done = f32[5,256,256]{1,2,0:T(8,128)} async-done(((f32[5,256,256]{1,2,0:T(8,128)}), f32[5,256,256]{1,2,0:T(8,128)}) %all-reduce.4.cloned.1.call-update) | async-done | bytes 1310736 | tf_op jit(solution)/shard_map/psum | solution.py:39
  210.4 1.9 fusion.22
  212.3 46.3 %psum.36 = f32[256,16]{0,1:T(8,128)S(1)} all-reduce(f32[256,16]{0,1:T(8,128)S(1)} %fusion.22), channel_id=1, replica_groups=mesh['row'=16,'col'=16] {'row'}, use_global_device_ids=true, to_apply=%region_2.0 | all-reduce | flops 4096 | bytes 32768 | tf_op jit(solution)/shard_map/psum | solution.py:48
  258.5 0.0 copy-done
  258.5 0.0 copy-start.1
  258.5 0.4 convolution_bitcast_fusion
  259.0 2.6 convolution_add_fusion
  261.6 1.2 pad_maximum_fusion
  262.8 0.0 copy-done.1
  262.9 0.0 copy-start.2
  262.9 0.0 all-reduce.6.cloned.1.call-update
  262.9 0.9 copy-done.2
  263.8 0.1 constant_dynamic-slice_fusion
  263.9 0.1 copy.57
  264.0 0.2 compare_reduce_fusion
  264.2 5.8 %fusion.8 = f32[5,256,256]{2,0,1:T(8,128)S(1)} fusion(f32[16,256,256]{2,1,0:T(8,128)} %all-gather.5.cloned.1.call-done, s32[16]{0:T(128)S(1)} %copy-done.4, s32[5]{0:T(128)S(1)} %fusion.63), kind=kOutput, calls=%fused_computation.8 | convolution fusion | flops 62914640 | bytes 5505108 | tf_op jit(solution)/shard_map/aj,jxy->axy/dot_general | solution.py:35
  270.0 1.6 fusion.31
  271.6 3.2 fusion.27
  274.9 86.3 %all-reduce.6.cloned.1.call-done = f32[6,256,256]{1,2,0:T(8,128)} async-done(((f32[6,256,256]{1,2,0:T(8,128)}), f32[6,256,256]{1,2,0:T(8,128)}) %all-reduce.6.cloned.1.call-update) | async-done | bytes 1572880 | tf_op jit(solution)/shard_map/psum | solution.py:39
  361.2 1.9 convolution_bitcast_fusion.1
  363.1 48.2 %all-reduce = (f32[16,16,16]{0,2,1:T(8,128)S(1)}, f32[256,16]{0,1:T(8,128)S(1)}) all-reduce(f32[16,16,16]{0,2,1:T(8,128)S(1)} %bitcast.78, f32[256,16]{0,1:T(8,128)S(1)} %convolution_bitcast_fusion.1), channel_id=1, replica_groups=mesh['row'=16,'col'=16] {'row'}, use_global_device_ids=true, to_apply=%region_5.0 | all-reduce | flops 8192 | bytes 65536 | tf_op jit(solution)/shard_map/psum | solution.py:67
  411.3 0.7 reshape.57
  412.0 5.9 %all-to-all-start = ((f32[16,1,256]{2,1,0:T(1,128)}), f32[16,1,256]{2,1,0:T(1,128)S(1)}, u32[]{:S(2)}, u32[]{:S(2)}) async-start(f32[16,1,256]{2,1,0:T(1,128)} %reshape.57), calls=%async_computation | async-start | bytes 32768 | tf_op jit(solution)/shard_map/all_to_all | solution.py:68
  417.9 1.6 multiply_bitcast_fusion
  419.5 4.6 %all-to-all-done = f32[16,1,256]{2,1,0:T(1,128)S(1)} async-done(((f32[16,1,256]{2,1,0:T(1,128)}), f32[16,1,256]{2,1,0:T(1,128)S(1)}, u32[]{:S(2)}, u32[]{:S(2)}) %all-to-all-start) | async-done | bytes 16416 | tf_op jit(solution)/shard_map/all_to_all | solution.py:68
  424.1 0.5 broadcast.23
  424.6 0.7 reduce
  425.3 0.1 reshape.58
  425.5 0.1 all_to_all.17
  425.6 1.3 fusion.39
  426.9 1.6 fusion.25
  (7 shorter events, 0.1 us)
Async XLA Ops:
  7.2 251.4 %copy-start = (f32[256,256]{1,0:T(8,128)S(1)}, f32[256,256]{1,0:T(8,128)}, u32[]{:S(2)}) copy-start(f32[256,256]{1,0:T(8,128)} %param.13) | copy-start | bytes 786436
  7.2 61.5 %all-gather.3.cloned.1.call-start = ((), (), s32[]{:S(2)}) async-start(), calls=%async_computation.1 | async-start | bytes 8912896 | tf_op jit(solution)/shard_map/all_gather | solution.py:31
  7.9 103.0 %all-gather.5.cloned.1.call-start = ((), (), s32[]{:S(2)}) async-start(), calls=%async_computation.3 | async-start | bytes 4456448 | tf_op jit(solution)/shard_map/all_gather | solution.py:31
  8.7 201.7 %all-reduce.4.cloned.1.call-start = ((), (), s32[]{:S(2)}) async-start(), calls=%async_computation.2 | async-start | bytes 2621440 | tf_op jit(solution)/shard_map/psum | solution.py:39
  80.8 30.1 %copy-start.4 = (s32[16]{0:T(128)S(1)}, s32[16]{0:T(128)}, u32[]{:S(2)}) copy-start(s32[16]{0:T(128)} %param.10) | copy-start | bytes 196
  90.8 270.4 %all-reduce.6.cloned.1.call-start = ((), (), s32[]{:S(2)}) async-start(), calls=%async_computation.4 | async-start | bytes 3145728 | tf_op jit(solution)/shard_map/psum | solution.py:39
  118.3 10.0 %copy-start.3 = (s32[32]{0:T(128)S(1)}, s32[32]{0:T(128)}, u32[]{:S(2)}) copy-start(s32[32]{0:T(128)} %param.9) | copy-start | bytes 388
  258.5 4.3 copy-start.1
  262.9 1.0 copy-start.2
  412.0 12.1 %all-to-all-start = ((f32[16,1,256]{2,1,0:T(1,128)}), f32[16,1,256]{2,1,0:T(1,128)S(1)}, u32[]{:S(2)}, u32[]{:S(2)}) async-start(f32[16,1,256]{2,1,0:T(1,128)} %reshape.57), calls=%async_computation | async-start | bytes 32768 | tf_op jit(solution)/shard_map/all_to_all | solution.py:68
Sparse Core Ops, SparseCore 0:
  9.8 58.7 all-gather.2
  70.5 40.4 all-gather.4
  114.2 96.1 all-reduce.3
  263.0 98.1 all-reduce.5
where the time goes:
time: 444 us; the launch traced here: 435 us
  waiting for transfers between devices  231 us (52%)
  blocking collectives  94.4 us (21%)
  matrix products  64.5 us (15%)
  starting transfers between devices  16.8 us (4%)
  between operations  14.3 us (3%)
  other arithmetic  7.53 us (2%)
  local copies, waits for them, and re-layouts  6.73 us (2%)
    psum x2, waiting for transfers between devices, reduce_cols(): summed = lax.psum(stacked, 'col')  158 us
    all_gather x2, waiting for transfers between devices, route(): block_in = lax.all_gather(factor, 'row', axis=0, tiled=True)  67.4 us
    psum x1, blocking collectives, body(): turned_sum, second_sum = lax.psum((turned_part, second_terms), 'row')  48.2 us
    psum x1, blocking collectives, body(): lax.psum(diag_terms, 'row')  46.3 us
    dot_general x2, matrix products, route(): row_sel = jnp.einsum('aj,jxy->axy', pick_row, block_in, precision=PRECISE)  16.6 us
    dot_general x2, matrix products, route(): col_sel = jnp.einsum('bj,jxy->bxy', pick_col, block_in, precision=PRECISE)  16.5 us
    psum x2, starting transfers between devices, reduce_cols(): summed = lax.psum(stacked, 'col')  10.8 us
    dot_general x1, matrix products, body(): jnp.einsum('abxy,byz->axz', local_inv, col_second, precision=PRECISE)  9.96 us
  transfers between devices with their start and end apart: 5, of which 5 were waited for; matrix products, arithmetic and copies ran while one was open for 15% of the time, Pallas kernels for 0%

commit v1 on v0

--- a/solution.py
+++ b/solution.py
@@ -36,7 +36,9 @@
         return (col_sel, row_sel)
 
     def reduce_cols(stacked):
-        summed = lax.psum(stacked, "col")
+        summed = stacked
+        for hop in (1, 2, 4, 8):
+            summed = summed + lax.ppermute(summed, "col", [(dev, dev ^ hop) for dev in range(16)])
         return lax.dynamic_slice_in_dim(summed, offset, col_width, 2)
 
     col_first, row_first = route(factor_first, struct_first)

time: 444 us -> 502 us (1.13)
  waiting for transfers between devices: 231 us -> 271 us
  starting transfers between devices: 16.8 us -> 36.4 us
  matrix products: 64.5 us -> 57.6 us
  blocking collectives: 94.4 us -> 101 us
    ppermute x0 -> x8, waiting for transfers between devices: none -> 204 us  [reduce_cols(): lax.ppermute(summed, 'col', [(dev, dev ^ hop) for dev in range(16)])]
    psum x2 -> x0, waiting for transfers between devices: 158 us -> none  [reduce_cols(): summed = lax.psum(stacked, 'col')]
    ppermute x0 -> x8, starting transfers between devices: none -> 29 us  [reduce_cols(): lax.ppermute(summed, 'col', [(dev, dev ^ hop) for dev in range(16)])]
    psum x2 -> x0, starting transfers between devices: 10.8 us -> none  [reduce_cols(): summed = lax.psum(stacked, 'col')]
    all_gather x2, waiting for transfers between devices: 67.4 us -> 60 us  [route(): block_in = lax.all_gather(factor, 'row', axis=0, tiled=True)]
    psum x1, blocking collectives: 48.2 us -> 54.8 us  [body(): turned_sum, second_sum = lax.psum((turned_part, second_terms), 'row')]
  transfers between devices with their start and end apart: 5 -> 11, of which waited for: 5 -> 10; matrix products, arithmetic and copies ran while one was open for 15% -> 12% of each run, Pallas kernels for 0% -> 0%
where the time goes in v1:
time: 502 us; the launch traced here: 493 us
  waiting for transfers between devices  271 us (54%)
  blocking collectives  101 us (20%)
  matrix products  57.6 us (11%)
  starting transfers between devices  36.4 us (7%)
  between operations  14.7 us (3%)
  other arithmetic  7.38 us (1%)
    ppermute x8, waiting for transfers between devices, reduce_cols(): lax.ppermute(summed, 'col', [(dev, dev ^ hop) for dev in range(16)])  204 us
    all_gather x2, waiting for transfers between devices, route(): block_in = lax.all_gather(factor, 'row', axis=0, tiled=True)  60 us
    psum x1, blocking collectives, body(): turned_sum, second_sum = lax.psum((turned_part, second_terms), 'row')  54.8 us
    psum x1, blocking collectives, body(): lax.psum(diag_terms, 'row')  45.9 us
    ppermute x8, starting transfers between devices, reduce_cols(): lax.ppermute(summed, 'col', [(dev, dev ^ hop) for dev in range(16)])  29 us
    dot_general x2, matrix products, route(): row_sel = jnp.einsum('aj,jxy->axy', pick_row, block_in, precision=PRECISE)  16.6 us
    dot_general x2, matrix products, route(): col_sel = jnp.einsum('bj,jxy->bxy', pick_col, block_in, precision=PRECISE)  16.5 us
  transfers between devices with their start and end apart: 11, of which 10 were waited for; matrix products, arithmetic and copies ran while one was open for 12% of the time, Pallas kernels for 0%

profile of v1, /device:TPU:2, one launch (start us, length us, event | category | flops | bytes accessed | tf_op | source)
XLA Modules:
  0.0 492.9 jit_solution(6123610381355474014)
XLA Ops:
  7.2 0.0 copy-start
  7.2 0.0 all-gather.3.cloned.1.call-start
  7.2 0.7 all-gather.3.cloned.1.call-update
  7.9 0.0 all-gather.5.cloned.1.call-start
  8.0 0.7 all-gather.5.cloned.1.call-update
  8.7 60.0 %all-gather.3.cloned.1.call-done = f32[32,256,256]{2,1,0:T(8,128)} async-done(((f32[2,256,256]{2,1,0:T(8,128)}), f32[32,256,256]{2,1,0:T(8,128)}) %all-gather.3.cloned.1.call-update) | async-done | bytes 8388624 | tf_op jit(solution)/shard_map/all_gather | solution.py:31
  68.6 10.6 %fusion.2 = f32[5,256,256]{2,0,1:T(8,128)S(1)} fusion(f32[32,256,256]{2,1,0:T(8,128)} %all-gather.3.cloned.1.call-done, s32[32]{0:T(128)} %param.9, s32[5]{0:T(128)S(1)} %fusion.58), kind=kOutput, calls=%fused_computation.2 | convolution fusion | flops 125829280 | bytes 9699476 | tf_op jit(solution)/shard_map/bj,jxy->bxy/dot_general | solution.py:34
  79.3 1.5 copy.31
  80.8 8.9 %fusion.12 = f32[5,256,256]{1,2,0:T(8,128)S(1)} fusion(f32[5,1,5,1,256,256]{5,4,3,2,1,0:T(8,128)} %param.8, f32[5,256,256]{1,2,0:T(8,128)} %copy.31), kind=kOutput, calls=%fused_computation.13 | convolution fusion | flops 5033164800 | bytes 9175040 | tf_op jit(solution)/shard_map/abxy,byz->axz/dot_general | solution.py:45
  89.7 0.6 collective-permute-start
  90.3 30.4 %collective-permute-done = f32[5,256,256]{1,2,0:T(8,128)S(1)} collective-permute-done((f32[5,256,256]{1,2,0:T(8,128)S(1)}, f32[5,256,256]{1,2,0:T(8,128)S(1)}, u32[]{:S(2)}, u32[]{:S(2)}) %collective-permute-start) | collective-permute-done | bytes 1310752 | tf_op jit(solution)/shard_map/ppermute | solution.py:41
  120.7 0.2 add.76
  120.9 0.0 copy-start.2
  120.9 0.0 copy-start.4
  120.9 13.9 %collective-permute-start.1 = (f32[5,256,256]{1,2,0:T(8,128)S(1)}, f32[5,256,256]{1,2,0:T(8,128)S(1)}, u32[]{:S(2)}, u32[]{:S(2)}) collective-permute-start(f32[5,256,256]{1,2,0:T(8,128)S(1)} %add.76), channel_id=1, source_target_pairs={{0,2},{1,3},{2,0},{3,1},{4,6},{5,7},{6,4},{7,5},{8,10},{9,11},{10,... | collective-permute-start | bytes 3932168 | tf_op jit(solution)/shard_map/ppermute | solution.py:41
  134.8 29.5 %collective-permute-done.1 = f32[5,256,256]{1,2,0:T(8,128)S(1)} collective-permute-done((f32[5,256,256]{1,2,0:T(8,128)S(1)}, f32[5,256,256]{1,2,0:T(8,128)S(1)}, u32[]{:S(2)}, u32[]{:S(2)}) %collective-permute-start.1) | collective-permute-done | bytes 1310752 | tf_op jit(solution)/shard_map/ppermute | solution.py:41
  164.3 0.2 add.77
  164.5 1.6 collective-permute-start.2
  166.0 0.1 constant_dynamic-slice_fusion.1
  166.1 0.1 copy.48
  166.2 0.2 compare_reduce_fusion.1
  166.4 27.3 %collective-permute-done.2 = f32[5,256,256]{1,2,0:T(8,128)S(1)} collective-permute-done((f32[5,256,256]{1,2,0:T(8,128)S(1)}, f32[5,256,256]{1,2,0:T(8,128)S(1)}, u32[]{:S(2)}, u32[]{:S(2)}) %collective-permute-start.2) | collective-permute-done | bytes 1310752 | tf_op jit(solution)/shard_map/ppermute | solution.py:41
  193.8 1.3 add.78
  195.1 3.0 collective-permute-start.3
  198.1 5.8 %fusion.10 = f32[5,256,256]{2,0,1:T(8,128)S(1)} fusion(f32[16,256,256]{2,1,0:T(8,128)} %all-gather.5.cloned.1.call-done, s32[16]{0:T(128)S(1)} %copy-done.5, s32[5]{0:T(128)S(1)} %fusion.58), kind=kOutput, calls=%fused_computation.10 | convolution fusion | flops 62914640 | bytes 5505108 | tf_op jit(solution)/shard_map/bj,jxy->bxy/dot_general | solution.py:34
  203.9 1.5 copy.36
  205.4 8.9 %fusion.15 = f32[5,256,256]{1,2,0:T(8,128)S(1)} fusion(f32[5,1,5,1,256,256]{5,4,3,2,1,0:T(8,128)} %param.8, f32[5,256,256]{1,2,0:T(8,128)} %copy.36), kind=kOutput, calls=%fused_computation.14 | convolution fusion | flops 5033164800 | bytes 9175040 | tf_op jit(solution)/shard_map/abxy,byz->axz/dot_general | solution.py:55
  214.3 10.6 %fusion = f32[5,256,256]{2,0,1:T(8,128)S(1)} fusion(f32[32,256,256]{2,1,0:T(8,128)} %all-gather.3.cloned.1.call-done, s32[32]{0:T(128)S(1)} %copy-done.4, s32[5]{0:T(128)S(1)} %fusion.59), kind=kOutput, calls=%fused_computation | convolution fusion | flops 125829280 | bytes 9699476 | tf_op jit(solution)/shard_map/aj,jxy->axy/dot_general | solution.py:35
  224.9 0.3 collective-permute-done.3
  225.2 1.6 multiply_bitcast_fusion.1
  226.9 1.0 fusion.22
  227.9 45.9 %psum.21 = f32[256,16]{0,1:T(8,128)S(1)} all-reduce(f32[256,16]{0,1:T(8,128)S(1)} %fusion.22), channel_id=1, replica_groups=mesh['row'=16,'col'=16] {'row'}, use_global_device_ids=true, to_apply=%region_1.0 | all-reduce | flops 4096 | bytes 32768 | tf_op jit(solution)/shard_map/psum | solution.py:50
  273.8 0.4 convolution_bitcast_fusion
  274.2 1.3 convolution_add_fusion
  275.5 0.2 pad_maximum_fusion
  275.7 0.6 collective-permute-start.4
  276.3 32.7 %collective-permute-done.4 = f32[6,256,256]{1,2,0:T(8,128)S(1)} collective-permute-done((f32[6,256,256]{1,2,0:T(8,128)S(1)}, f32[6,256,256]{1,2,0:T(8,128)S(1)}, u32[]{:S(2)}, u32[]{:S(2)}) %collective-permute-start.4) | collective-permute-done | bytes 1572896 | tf_op jit(solution)/shard_map/ppermute | solution.py:41
  309.0 0.2 fusion.60
  309.2 3.8 collective-permute-start.5
  313.0 30.7 %collective-permute-done.5 = f32[6,256,256]{1,2,0:T(8,128)S(1)} collective-permute-done((f32[6,256,256]{1,2,0:T(8,128)S(1)}, f32[6,256,256]{1,2,0:T(8,128)S(1)}, u32[]{:S(2)}, u32[]{:S(2)}) %collective-permute-start.5) | collective-permute-done | bytes 1572896 | tf_op jit(solution)/shard_map/ppermute | solution.py:41
  343.6 0.2 add.84
  343.9 1.6 collective-permute-start.6
  345.4 31.3 %collective-permute-done.6 = f32[6,256,256]{1,2,0:T(8,128)S(1)} collective-permute-done((f32[6,256,256]{1,2,0:T(8,128)S(1)}, f32[6,256,256]{1,2,0:T(8,128)S(1)}, u32[]{:S(2)}, u32[]{:S(2)}) %collective-permute-start.6) | collective-permute-done | bytes 1572896 | tf_op jit(solution)/shard_map/ppermute | solution.py:41
  376.8 0.2 add.85
  377.0 3.9 collective-permute-start.7
  380.9 0.1 constant_dynamic-slice_fusion
  381.0 0.1 copy.49
  381.0 0.2 compare_reduce_fusion
  381.2 5.9 %fusion.8 = f32[5,256,256]{2,0,1:T(8,128)S(1)} fusion(f32[16,256,256]{2,1,0:T(8,128)} %all-gather.5.cloned.1.call-done, s32[16]{0:T(128)S(1)} %copy-done.5, s32[5]{0:T(128)S(1)} %fusion.59), kind=kOutput, calls=%fused_computation.8 | convolution fusion | flops 62914640 | bytes 5505108 | tf_op jit(solution)/shard_map/aj,jxy->axy/dot_general | solution.py:35
  387.2 2.3 fusion.27
  389.5 22.2 %collective-permute-done.7 = f32[6,256,256]{1,2,0:T(8,128)} collective-permute-done((f32[6,256,256]{1,2,0:T(8,128)S(1)}, f32[6,256,256]{1,2,0:T(8,128)}, u32[]{:S(2)}, u32[]{:S(2)}) %collective-permute-start.7) | collective-permute-done | bytes 1572896 | tf_op jit(solution)/shard_map/ppermute | solution.py:41
  411.7 0.9 dynamic-slice_add_fusion
  412.6 1.0 convolution_bitcast_fusion.1
  413.6 54.8 %all-reduce = (f32[16,16,16]{0,2,1:T(8,128)S(1)}, f32[256,16]{0,1:T(8,128)S(1)}) all-reduce(f32[16,16,16]{0,2,1:T(8,128)S(1)} %bitcast.79, f32[256,16]{0,1:T(8,128)S(1)} %convolution_bitcast_fusion.1), channel_id=1, replica_groups=mesh['row'=16,'col'=16] {'row'}, use_global_device_ids=true, to_apply=%region_3.0 | all-reduce | flops 8192 | bytes 65536 | tf_op jit(solution)/shard_map/psum | solution.py:69
  468.4 0.7 reshape.57
  469.2 7.3 %all-to-all-start = ((f32[16,1,256]{2,1,0:T(1,128)}), f32[16,1,256]{2,1,0:T(1,128)S(1)}, u32[]{:S(2)}, u32[]{:S(2)}) async-start(f32[16,1,256]{2,1,0:T(1,128)} %reshape.57), calls=%async_computation | async-start | bytes 32768 | tf_op jit(solution)/shard_map/all_to_all | solution.py:70
  476.5 0.7 multiply_bitcast_fusion
  477.2 5.5 %all-to-all-done = f32[16,1,256]{2,1,0:T(1,128)S(1)} async-done(((f32[16,1,256]{2,1,0:T(1,128)}), f32[16,1,256]{2,1,0:T(1,128)S(1)}, u32[]{:S(2)}, u32[]{:S(2)}) %all-to-all-start) | async-done | bytes 16416 | tf_op jit(solution)/shard_map/all_to_all | solution.py:70
  482.7 0.5 broadcast.23
  483.2 0.7 reduce
  483.9 0.1 reshape.58
  484.1 0.1 all_to_all.17
  484.2 0.6 fusion.39
  484.8 0.8 fusion.25
  (17 shorter events, 0.1 us)
Async XLA Ops:
  7.2 266.6 %copy-start = (f32[256,256]{1,0:T(8,128)S(1)}, f32[256,256]{1,0:T(8,128)}, u32[]{:S(2)}) copy-start(f32[256,256]{1,0:T(8,128)} %param.13) | copy-start | bytes 786436
  7.2 61.5 %all-gather.3.cloned.1.call-start = ((), (), s32[]{:S(2)}) async-start(), calls=%async_computation.1 | async-start | bytes 8912896 | tf_op jit(solution)/shard_map/all_gather | solution.py:31
  7.9 190.2 %all-gather.5.cloned.1.call-start = ((), (), s32[]{:S(2)}) async-start(), calls=%async_computation.2 | async-start | bytes 4456448 | tf_op jit(solution)/shard_map/all_gather | solution.py:31
  89.7 31.0 %collective-permute-start = (f32[5,256,256]{1,2,0:T(8,128)S(1)}, f32[5,256,256]{1,2,0:T(8,128)S(1)}, u32[]{:S(2)}, u32[]{:S(2)}) collective-permute-start(f32[5,256,256]{1,2,0:T(8,128)S(1)} %fusion.12), channel_id=1, source_target_pairs={{0,1},{1,0},{2,3},{3,2},{4,5},{5,4},{6,7},{7,6},{8,9},{9,8},{10,11... | collective-permute-start | bytes 3932168 | tf_op jit(solution)/shard_map/ppermute | solution.py:41
  120.9 45.2 %copy-start.2 = (f32[256,256]{1,0:T(8,128)S(1)}, f32[256,256]{1,0:T(8,128)}, u32[]{:S(2)}) copy-start(f32[256,256]{1,0:T(8,128)} %param.14) | copy-start | bytes 786436
  120.9 45.3 %copy-start.4 = (s32[32]{0:T(128)S(1)}, s32[32]{0:T(128)}, u32[]{:S(2)}) copy-start(s32[32]{0:T(128)} %param.9) | copy-start | bytes 388
  120.9 43.4 %collective-permute-start.1 = (f32[5,256,256]{1,2,0:T(8,128)S(1)}, f32[5,256,256]{1,2,0:T(8,128)S(1)}, u32[]{:S(2)}, u32[]{:S(2)}) collective-permute-start(f32[5,256,256]{1,2,0:T(8,128)S(1)} %add.76), channel_id=1, source_target_pairs={{0,2},{1,3},{2,0},{3,1},{4,6},{5,7},{6,4},{7,5},{8,10},{9,11},{10,... | collective-permute-start | bytes 3932168 | tf_op jit(solution)/shard_map/ppermute | solution.py:41
  164.5 29.3 %collective-permute-start.2 = (f32[5,256,256]{1,2,0:T(8,128)S(1)}, f32[5,256,256]{1,2,0:T(8,128)S(1)}, u32[]{:S(2)}, u32[]{:S(2)}) collective-permute-start(f32[5,256,256]{1,2,0:T(8,128)S(1)} %add.77), channel_id=1, source_target_pairs={{0,4},{1,5},{2,6},{3,7},{4,0},{5,1},{6,2},{7,3},{8,12},{9,13},{10,... | collective-permute-start | bytes 3932168 | tf_op jit(solution)/shard_map/ppermute | solution.py:41
  166.4 31.7 %copy-start.5 = (s32[16]{0:T(128)S(1)}, s32[16]{0:T(128)}, u32[]{:S(2)}) copy-start(s32[16]{0:T(128)} %param.10) | copy-start | bytes 196
  195.1 30.2 %collective-permute-start.3 = (f32[5,256,256]{1,2,0:T(8,128)}, f32[5,256,256]{1,2,0:T(8,128)}, u32[]{:S(2)}, u32[]{:S(2)}) collective-permute-start(f32[5,256,256]{1,2,0:T(8,128)} %add.78), channel_id=1, source_target_pairs={{0,8},{1,9},{2,10},{3,11},{4,12},{5,13},{6,14},{7,15},{8,0},{9,1},... | collective-permute-start | bytes 3932168 | tf_op jit(solution)/shard_map/ppermute | solution.py:41
  273.7 1.9 copy-start.1
  275.7 33.3 %collective-permute-start.4 = (f32[6,256,256]{1,2,0:T(8,128)S(1)}, f32[6,256,256]{1,2,0:T(8,128)S(1)}, u32[]{:S(2)}, u32[]{:S(2)}) collective-permute-start(f32[6,256,256]{1,2,0:T(8,128)S(1)} %pad_maximum_fusion), channel_id=1, source_target_pairs={{0,1},{1,0},{2,3},{3,2},{4,5},{5,4},{6,7},{7,6},{8,9},{9,8},{10,11... | collective-permute-start | bytes 4718600 | tf_op jit(solution)/shard_map/ppermute | solution.py:41
  309.2 34.4 %collective-permute-start.5 = (f32[6,256,256]{1,2,0:T(8,128)S(1)}, f32[6,256,256]{1,2,0:T(8,128)S(1)}, u32[]{:S(2)}, u32[]{:S(2)}) collective-permute-start(f32[6,256,256]{1,2,0:T(8,128)S(1)} %fusion.60), channel_id=1, source_target_pairs={{0,2},{1,3},{2,0},{3,1},{4,6},{5,7},{6,4},{7,5},{8,10},{9,11},{10,... | collective-permute-start | bytes 4718600 | tf_op jit(solution)/shard_map/ppermute | solution.py:41
  343.8 37.0 %copy-start.3 = (f32[256,256]{1,0:T(8,128)S(1)}, f32[256,256]{1,0:T(8,128)}, u32[]{:S(2)}) copy-start(f32[256,256]{1,0:T(8,128)} %param.15) | copy-start | bytes 786436
  343.9 32.9 %collective-permute-start.6 = (f32[6,256,256]{1,2,0:T(8,128)S(1)}, f32[6,256,256]{1,2,0:T(8,128)S(1)}, u32[]{:S(2)}, u32[]{:S(2)}) collective-permute-start(f32[6,256,256]{1,2,0:T(8,128)S(1)} %add.84), channel_id=1, source_target_pairs={{0,4},{1,5},{2,6},{3,7},{4,0},{5,1},{6,2},{7,3},{8,12},{9,13},{10,... | collective-permute-start | bytes 4718600 | tf_op jit(solution)/shard_map/ppermute | solution.py:41
  377.0 34.7 %collective-permute-start.7 = (f32[6,256,256]{1,2,0:T(8,128)S(1)}, f32[6,256,256]{1,2,0:T(8,128)}, u32[]{:S(2)}, u32[]{:S(2)}) collective-permute-start(f32[6,256,256]{1,2,0:T(8,128)S(1)} %add.85), channel_id=1, source_target_pairs={{0,8},{1,9},{2,10},{3,11},{4,12},{5,13},{6,14},{7,15},{8,0},{9,1},... | collective-permute-start | bytes 4718600 | tf_op jit(solution)/shard_map/ppermute | solution.py:41
  469.2 13.5 %all-to-all-start = ((f32[16,1,256]{2,1,0:T(1,128)}), f32[16,1,256]{2,1,0:T(1,128)S(1)}, u32[]{:S(2)}, u32[]{:S(2)}) async-start(f32[16,1,256]{2,1,0:T(1,128)} %reshape.57), calls=%async_computation | async-start | bytes 32768 | tf_op jit(solution)/shard_map/all_to_all | solution.py:70
Sparse Core Ops, SparseCore 0:
  9.8 58.7 all-gather.2
  70.5 40.4 all-gather.4
